TPU v7x, 512 devices: a whole 4x8x8 slice. The times are simulated.
512 devices in a mesh: rep: 8 (over y), exp: 64 (over x, z, core).
Axes of the slice: x: 4, y: 8, z: 8, core: 2. Of those that a mesh axis runs over, the one named last changes fastest.
Arguments:
- tokens: bfloat16 [65536, 1024], P(('rep', 'exp')), may hold values from -6 to 6
- cotangent: bfloat16 [65536, 1024], P(('rep', 'exp')), may hold values from -6 to 6
- expert_ids: int32 [65536, 2], P(('rep', 'exp')), may hold values from 0 to 63, all different within a row; in each aligned block of 128 rows (0 to 127, 128 to 255, ...) at most 8 rows name the same one
- combine_weight: float32 [65536, 2], P(('rep', 'exp')), may hold values from 0.2 to 1
- gate_weight: bfloat16 [64, 1024, 768], P('exp', 'rep'), may hold values from -0.1875 to 0.1875
- up_weight: bfloat16 [64, 1024, 768], P('exp', 'rep'), may hold values from -0.1875 to 0.1875
- down_weight: bfloat16 [64, 768, 1024], P('exp', None, 'rep'), may hold values from -0.21875 to 0.21875
Outputs:
- mixed: bfloat16 [65536, 1024], P(('rep', 'exp'))
- token_grad: bfloat16 [65536, 1024], P(('rep', 'exp'))
- gate_grad: bfloat16 [64, 1024, 768], P('exp', 'rep')
- up_grad: bfloat16 [64, 1024, 768], P('exp', 'rep')
- down_grad: bfloat16 [64, 768, 1024], P('exp', None, 'rep')
Inputs may be any that keep to these rules, and one draw needn't show every extreme that they name: `expert_ids`: each token names 2 different experts. Among the 128 tokens of one aligned block of rows, no expert is named more than 8 times, and in some block an expert is named exactly 8 times.
All inputs are finite; a program needn't handle non-finite values.
Results may differ from a plain program's by a relative error of at most 0.014.
Values may be sent and summed in bfloat16 or wider, within the bound.
No kernel may reach another device: no remote copies, remote signals or barrier semaphores. Data moves between devices by JAX's collectives and lax.ppermute only.
A program may use at most 64 MiB of HBM per device.

v0:
```python
import jax
import jax.numpy as jnp
from jax import lax
from jax.sharding import PartitionSpec as P


def slot_rows(block_ids, expert_count, capacity):
    flat = block_ids.reshape(-1)
    onehot = (flat[:, None] == jnp.arange(expert_count, dtype=jnp.int32)[None, :]).astype(jnp.int32)
    before = jnp.cumsum(onehot, axis=0) - onehot
    return flat * capacity + jnp.sum(before * onehot, axis=1)


def expert_forward(block_x, w_gate, w_up, w_down):
    gate_value = jnp.dot(block_x, w_gate, preferred_element_type=jnp.float32)
    up_value = jnp.dot(block_x, w_up, preferred_element_type=jnp.float32)
    swish_value = jax.nn.silu(gate_value)
    hidden = (swish_value * up_value).astype(jnp.bfloat16)
    output = jnp.dot(hidden, w_down, preferred_element_type=jnp.float32).astype(jnp.bfloat16)
    return (gate_value, up_value, swish_value, hidden, output)


def average_rows(received, replicas):
    features, hidden_units = received.shape
    stacked = received.reshape(replicas, features // replicas, hidden_units).astype(jnp.float32)
    return (jnp.sum(stacked, axis=0) / replicas).astype(jnp.bfloat16)


def per_device(tokens, cotangent, expert_ids, combine_weight, gate_weight, up_weight, down_weight):
    tok_rows, features = tokens.shape
    top_count = expert_ids.shape[1]
    groups = lax.axis_size("exp")
    replicas = lax.axis_size("rep")
    capacity = 2 * tok_rows * top_count // groups
    pair_count = tok_rows * top_count
    destination = slot_rows(expert_ids, groups, capacity)
    x_pairs = jnp.repeat(tokens, top_count, axis=0)
    cot_pairs = (combine_weight[:, :, None] * cotangent[:, None, :].astype(jnp.float32)).astype(
        jnp.bfloat16
    )
    cot_pairs = cot_pairs.reshape(pair_count, features)
    send_rows = jnp.zeros((groups * capacity, features), jnp.bfloat16).at[destination].set(x_pairs)
    send_cot = jnp.zeros((groups * capacity, features), jnp.bfloat16).at[destination].set(cot_pairs)
    w_gate, w_up, w_down = (
        lax.all_gather(gate_weight[0], "rep", axis=0, tiled=True),
        lax.all_gather(up_weight[0], "rep", axis=0, tiled=True),
        lax.all_gather(down_weight[0], "rep", axis=1, tiled=True),
    )
    recv_rows, recv_cot = (
        lax.all_to_all(send_rows, "exp", split_axis=0, concat_axis=0, tiled=True),
        lax.all_to_all(send_cot, "exp", split_axis=0, concat_axis=0, tiled=True),
    )
    gate_value, up_value, swish_value, hidden, output = expert_forward(
        recv_rows, w_gate, w_up, w_down
    )
    grad_hidden = lax.dot_general(
        recv_cot, w_down, (((1,), (1,)), ((), ())), preferred_element_type=jnp.float32
    )
    sigma = jax.nn.sigmoid(gate_value)
    grad_gate = (grad_hidden * up_value * sigma * (1.0 + gate_value * (1.0 - sigma))).astype(
        jnp.bfloat16
    )
    grad_up = (grad_hidden * swish_value).astype(jnp.bfloat16)
    grad_rows = (
        lax.dot_general(
            grad_gate, w_gate, (((1,), (1,)), ((), ())), preferred_element_type=jnp.float32
        )
        + lax.dot_general(
            grad_up, w_up, (((1,), (1,)), ((), ())), preferred_element_type=jnp.float32
        )
    ).astype(jnp.bfloat16)
    back_out, back_grad = (
        lax.all_to_all(output, "exp", split_axis=0, concat_axis=0, tiled=True),
        lax.all_to_all(grad_rows, "exp", split_axis=0, concat_axis=0, tiled=True),
    )
    part_gate = lax.dot_general(
        recv_rows, grad_gate, (((0,), (0,)), ((), ())), preferred_element_type=jnp.float32
    ).astype(jnp.bfloat16)
    part_up = lax.dot_general(
        recv_rows, grad_up, (((0,), (0,)), ((), ())), preferred_element_type=jnp.float32
    ).astype(jnp.bfloat16)
    part_down = lax.dot_general(
        recv_cot, hidden, (((0,), (0,)), ((), ())), preferred_element_type=jnp.float32
    ).astype(jnp.bfloat16)
    red_gate, red_up, red_down = (
        lax.all_to_all(part_gate, "rep", split_axis=0, concat_axis=0, tiled=True),
        lax.all_to_all(part_up, "rep", split_axis=0, concat_axis=0, tiled=True),
        lax.all_to_all(part_down, "rep", split_axis=0, concat_axis=0, tiled=True),
    )
    gate_grad = average_rows(red_gate, replicas)[None]
    up_grad = average_rows(red_up, replicas)[None]
    down_grad = average_rows(red_down, replicas).T[None]
    out_pairs = back_out[destination].reshape(tok_rows, top_count, features).astype(jnp.float32)
    mixed = jnp.sum(combine_weight[:, :, None] * out_pairs, axis=1).astype(jnp.bfloat16)
    grad_pairs = back_grad[destination].reshape(tok_rows, top_count, features).astype(jnp.float32)
    token_grad = jnp.sum(grad_pairs, axis=1).astype(jnp.bfloat16)
    return (mixed, token_grad, gate_grad, up_grad, down_grad)


def solution(mesh):
    placed = (
        P(("rep", "exp"), None),
        P(("rep", "exp"), None),
        P(("rep", "exp"), None),
        P(("rep", "exp"), None),
        P("exp", "rep", None),
        P("exp", "rep", None),
        P("exp", None, "rep"),
    )
    return jax.shard_map(
        per_device,
        mesh=mesh,
        in_specs=placed,
        out_specs=(
            P(("rep", "exp"), None),
            P(("rep", "exp"), None),
            P("exp", "rep", None),
            P("exp", "rep", None),
            P("exp", None, "rep"),
        ),
        check_vma=False,
    )
```

profile of v0, /device:TPU:1, one launch (start us, length us, event | category | flops | bytes accessed | tf_op | source)
XLA Modules:
  0.0 371.4 jit_solution(11726433471744356704)
XLA Ops:
  7.2 0.7 all-gather.9.cloned.1.call-update
  7.9 0.7 all-gather.7.cloned.1.call-update
  8.6 0.8 copy.15
  9.7 0.6 reduce-window.6
  10.6 0.7 broadcast_multiply_fusion
  11.5 1.2 broadcast_in_dim.4
  12.8 0.2 reshape.141
  13.1 2.7 scatter_custom_fusion
  15.8 14.8 %all-to-all-start = ((bf16[64,8,1024]{2,1,0:T(8,128)(2,1)}), bf16[64,8,1024]{2,1,0:T(8,128)(2,1)S(1)}, u32[]{:S(2)}, u32[]{:S(2)}) async-start(bf16[64,8,1024]{2,1,0:T(8,128)(2,1)} %bitcast.3), calls=%async_computation | async-start | bytes 2097152 | tf_op jit(solution)/shard_map/all_to_all | solution.py:50
  30.7 0.7 all-gather.11.cloned.1.call-update
  31.7 0.3 mul.77
  31.9 0.7 mul.78
  32.7 2.8 scatter_custom_fusion.1
  35.5 23.7 %all-to-all-done = bf16[64,8,1024]{2,1,0:T(8,128)(2,1)S(1)} async-done(((bf16[64,8,1024]{2,1,0:T(8,128)(2,1)}), bf16[64,8,1024]{2,1,0:T(8,128)(2,1)S(1)}, u32[]{:S(2)}, u32[]{:S(2)}) %all-to-all-start) | async-done | bytes 1048608 | tf_op jit(solution)/shard_map/all_to_all | solution.py:50
  59.2 6.2 %all-to-all-start.2 = ((bf16[64,8,1024]{2,1,0:T(8,128)(2,1)}), bf16[64,8,1024]{2,1,0:T(8,128)(2,1)S(1)}, u32[]{:S(2)}, u32[]{:S(2)}) async-start(bf16[64,8,1024]{2,1,0:T(8,128)(2,1)} %bitcast.10), calls=%async_computation.2 | async-start | bytes 2097152 | tf_op jit(solution)/shard_map/all_to_all | solution.py:51
  65.4 3.5 fusion.5
  69.0 28.5 %all-gather.7.cloned.1.call-done = bf16[1,1024,768]{2,1,0:T(8,128)(2,1)} async-done(((bf16[1,128,768]{2,1,0:T(8,128)(2,1)}), bf16[1,1024,768]{2,1,0:T(8,128)(2,1)}) %all-gather.7.cloned.1.call-update) | async-done | bytes 1572880 | tf_op jit(solution)/shard_map/all_gather | solution.py:45
  97.5 3.5 fusion.9
  101.0 43.9 %all-gather.11.cloned.1.call-done = bf16[1,768,1024]{2,1,0:T(8,128)(2,1)} async-done(((bf16[1,768,128]{2,1,0:T(8,128)(2,1)}), bf16[1,768,1024]{2,1,0:T(8,128)(2,1)}) %all-gather.11.cloned.1.call-update) | async-done | bytes 1572880 | tf_op jit(solution)/shard_map/all_gather | solution.py:47
  145.0 4.9 %multiply_convert_fusion = (bf16[512,768]{1,0:T(8,128)(2,1)S(1)}, bf16[512,768]{1,0:T(8,128)(2,1)S(1)}, bf16[512,768]{1,0:T(8,128)(2,1)}) fusion(f32[512,768]{1,0:T(8,128)} %fusion.9, f32[512,768]{1,0:T(8,128)} %fusion.5, bf16[1,768,1024]{2,1,0:T(8,128)(2,1)} %all-gather.11.cloned.1.call-done, bf16[64,8,1024]{2,1,0:T(8,128)(2,1)S(1)} %all-to-all-done.2), kind=kOutput, calls=%fused_computation.22 | convolution fusion | flops 811204608 | bytes 8126464 | tf_op jit(solution)/shard_map/dot_general | solution.py:56
  149.9 1.0 fusion.7
  151.0 0.8 copy-done.4
  151.9 2.0 fusion.18
  153.9 15.0 %all-to-all-start.3 = ((bf16[64,8,1024]{2,1,0:T(8,128)(2,1)}), bf16[64,8,1024]{2,1,0:T(8,128)(2,1)S(1)}, u32[]{:S(2)}, u32[]{:S(2)}) async-start(bf16[64,8,1024]{2,1,0:T(8,128)(2,1)} %fusion.18), calls=%async_computation.3 | async-start | bytes 2097152 | tf_op jit(solution)/shard_map/all_to_all | solution.py:74
  168.9 3.4 fusion.15
  172.2 25.2 %all-to-all-done.3 = bf16[64,8,1024]{2,1,0:T(8,128)(2,1)S(1)} async-done(((bf16[64,8,1024]{2,1,0:T(8,128)(2,1)}), bf16[64,8,1024]{2,1,0:T(8,128)(2,1)S(1)}, u32[]{:S(2)}, u32[]{:S(2)}) %all-to-all-start.3) | async-done | bytes 1048608 | tf_op jit(solution)/shard_map/all_to_all | solution.py:74
  197.4 6.2 %all-to-all-start.1 = ((bf16[64,8,1024]{2,1,0:T(8,128)(2,1)}), bf16[64,8,1024]{2,1,0:T(8,128)(2,1)S(1)}, u32[]{:S(2)}, u32[]{:S(2)}) async-start(bf16[64,8,1024]{2,1,0:T(8,128)(2,1)} %fusion.15), calls=%async_computation.1 | async-start | bytes 2097152 | tf_op jit(solution)/shard_map/all_to_all | solution.py:73
  203.6 3.3 convolution_convert_fusion.2
  206.9 25.2 %all-to-all-done.1 = bf16[64,8,1024]{2,1,0:T(8,128)(2,1)S(1)} async-done(((bf16[64,8,1024]{2,1,0:T(8,128)(2,1)}), bf16[64,8,1024]{2,1,0:T(8,128)(2,1)S(1)}, u32[]{:S(2)}, u32[]{:S(2)}) %all-to-all-start.1) | async-done | bytes 1048608 | tf_op jit(solution)/shard_map/all_to_all | solution.py:73
  232.2 4.3 %all-to-all-start.4 = ((bf16[8,128,768]{2,1,0:T(8,128)(2,1)}), bf16[8,128,768]{2,1,0:T(8,128)(2,1)}, u32[]{:S(2)}, u32[]{:S(2)}) async-start(bf16[8,128,768]{2,1,0:T(8,128)(2,1)} %bitcast.89), calls=%async_computation.4 | async-start | bytes 3145728 | tf_op jit(solution)/shard_map/all_to_all | solution.py:86
  236.4 3.3 convolution_convert_fusion.1
  239.8 37.2 %all-to-all-done.4 = bf16[8,128,768]{2,1,0:T(8,128)(2,1)} async-done(((bf16[8,128,768]{2,1,0:T(8,128)(2,1)}), bf16[8,128,768]{2,1,0:T(8,128)(2,1)}, u32[]{:S(2)}, u32[]{:S(2)}) %all-to-all-start.4) | async-done | bytes 1572896 | tf_op jit(solution)/shard_map/all_to_all | solution.py:86
  277.0 4.4 %all-to-all-start.5 = ((bf16[8,128,768]{2,1,0:T(8,128)(2,1)}), bf16[8,128,768]{2,1,0:T(8,128)(2,1)}, u32[]{:S(2)}, u32[]{:S(2)}) async-start(bf16[8,128,768]{2,1,0:T(8,128)(2,1)} %bitcast.88), calls=%async_computation.5 | async-start | bytes 3145728 | tf_op jit(solution)/shard_map/all_to_all | solution.py:87
  281.4 3.3 convolution_convert_fusion
  284.7 34.9 %all-to-all-done.5 = bf16[8,128,768]{2,1,0:T(8,128)(2,1)} async-done(((bf16[8,128,768]{2,1,0:T(8,128)(2,1)}), bf16[8,128,768]{2,1,0:T(8,128)(2,1)}, u32[]{:S(2)}, u32[]{:S(2)}) %all-to-all-start.5) | async-done | bytes 1572896 | tf_op jit(solution)/shard_map/all_to_all | solution.py:87
  319.7 4.5 %all-to-all-start.6 = ((bf16[8,128,768]{2,1,0:T(8,128)(2,1)}), bf16[8,128,768]{2,1,0:T(8,128)(2,1)}, u32[]{:S(2)}, u32[]{:S(2)}) async-start(bf16[8,128,768]{2,1,0:T(8,128)(2,1)} %bitcast.87), calls=%async_computation.6 | async-start | bytes 3145728 | tf_op jit(solution)/shard_map/all_to_all | solution.py:88
  324.2 1.2 gather_fusion.1
  325.6 2.1 reduce_sum.62
  327.7 1.2 gather_fusion
  328.8 0.7 reshape.120
  329.5 2.1 multiply_reduce_fusion
  331.6 1.7 convert_reduce_fusion.2
  333.2 1.7 convert_reduce_fusion.1
  334.9 0.7 fusion.32
  335.6 0.7 fusion.33
  336.3 26.1 %all-to-all-done.6 = bf16[8,128,768]{2,1,0:T(8,128)(2,1)} async-done(((bf16[8,128,768]{2,1,0:T(8,128)(2,1)}), bf16[8,128,768]{2,1,0:T(8,128)(2,1)}, u32[]{:S(2)}, u32[]{:S(2)}) %all-to-all-start.6) | async-done | bytes 1572896 | tf_op jit(solution)/shard_map/all_to_all | solution.py:88
  362.4 1.7 convert_reduce_fusion
  364.1 0.8 copy.19
  (37 shorter events, 1.6 us)
Async XLA Ops:
  7.2 58.3 %all-gather.9.cloned.1.call-start = ((), (), s32[]{:S(2)}) async-start(), calls=%async_computation.8 | async-start | bytes 1769472 | tf_op jit(solution)/shard_map/all_gather | solution.py:46
  7.9 89.6 %all-gather.7.cloned.1.call-start = ((), (), s32[]{:S(2)}) async-start(), calls=%async_computation.7 | async-start | bytes 1769472 | tf_op jit(solution)/shard_map/all_gather | solution.py:45
  13.1 18.3 %copy-start.3 = (f32[128,2]{0,1:T(2,128)S(1)}, f32[128,2]{0,1:T(2,128)}, u32[]{:S(2)}) copy-start(f32[128,2]{0,1:T(2,128)} %param.10) | copy-start | bytes 3076
  13.1 18.6 %copy-start.2 = (bf16[128,1024]{1,0:T(8,128)(2,1)S(1)}, bf16[128,1024]{1,0:T(8,128)(2,1)}, u32[]{:S(2)}) copy-start(bf16[128,1024]{1,0:T(8,128)(2,1)} %param.8) | copy-start | bytes 786436
  15.8 43.4 %all-to-all-start = ((bf16[64,8,1024]{2,1,0:T(8,128)(2,1)}), bf16[64,8,1024]{2,1,0:T(8,128)(2,1)S(1)}, u32[]{:S(2)}, u32[]{:S(2)}) async-start(bf16[64,8,1024]{2,1,0:T(8,128)(2,1)} %bitcast.3), calls=%async_computation | async-start | bytes 2097152 | tf_op jit(solution)/shard_map/all_to_all | solution.py:50
  30.6 114.3 %all-gather.11.cloned.1.call-start = ((), (), s32[]{:S(2)}) async-start(), calls=%async_computation.9 | async-start | bytes 1769472 | tf_op jit(solution)/shard_map/all_gather | solution.py:47
  59.2 41.8 %all-to-all-start.2 = ((bf16[64,8,1024]{2,1,0:T(8,128)(2,1)}), bf16[64,8,1024]{2,1,0:T(8,128)(2,1)S(1)}, u32[]{:S(2)}, u32[]{:S(2)}) async-start(bf16[64,8,1024]{2,1,0:T(8,128)(2,1)} %bitcast.10), calls=%async_computation.2 | async-start | bytes 2097152 | tf_op jit(solution)/shard_map/all_to_all | solution.py:51
  101.0 48.9 %copy-start = (bf16[64,8,1024]{2,1,0:T(8,128)(2,1)}, bf16[64,8,1024]{2,1,0:T(8,128)(2,1)S(1)}, u32[]{:S(2)}) copy-start(bf16[64,8,1024]{2,1,0:T(8,128)(2,1)S(1)} %all-to-all-done.2) | copy-start | bytes 3145732
  145.0 4.9 %copy-start.5 = (bf16[1,1024,768]{2,1,0:T(8,128)(2,1)S(1)}, bf16[1,1024,768]{2,1,0:T(8,128)(2,1)}, u32[]{:S(2)}) copy-start(bf16[1,1024,768]{2,1,0:T(8,128)(2,1)} %all-gather.7.cloned.1.call-done) | copy-start | bytes 4718596
  149.9 1.0 copy-start.7
  149.9 1.1 copy-start.6
  149.9 2.0 copy-start.4
  153.9 15.0 %copy-start.8 = (bf16[512,768]{1,0:T(8,128)(2,1)S(1)}, bf16[512,768]{1,0:T(8,128)(2,1)}, u32[]{:S(2)}) copy-start(bf16[512,768]{1,0:T(8,128)(2,1)} %get-tuple-element.12) | copy-start | bytes 2359300
  153.9 43.5 %all-to-all-start.3 = ((bf16[64,8,1024]{2,1,0:T(8,128)(2,1)}), bf16[64,8,1024]{2,1,0:T(8,128)(2,1)S(1)}, u32[]{:S(2)}, u32[]{:S(2)}) async-start(bf16[64,8,1024]{2,1,0:T(8,128)(2,1)} %fusion.18), calls=%async_computation.3 | async-start | bytes 2097152 | tf_op jit(solution)/shard_map/all_to_all | solution.py:74
  197.4 34.8 %all-to-all-start.1 = ((bf16[64,8,1024]{2,1,0:T(8,128)(2,1)}), bf16[64,8,1024]{2,1,0:T(8,128)(2,1)S(1)}, u32[]{:S(2)}, u32[]{:S(2)}) async-start(bf16[64,8,1024]{2,1,0:T(8,128)(2,1)} %fusion.15), calls=%async_computation.1 | async-start | bytes 2097152 | tf_op jit(solution)/shard_map/all_to_all | solution.py:73
  232.2 44.8 %all-to-all-start.4 = ((bf16[8,128,768]{2,1,0:T(8,128)(2,1)}), bf16[8,128,768]{2,1,0:T(8,128)(2,1)}, u32[]{:S(2)}, u32[]{:S(2)}) async-start(bf16[8,128,768]{2,1,0:T(8,128)(2,1)} %bitcast.89), calls=%async_computation.4 | async-start | bytes 3145728 | tf_op jit(solution)/shard_map/all_to_all | solution.py:86
  277.0 4.5 %copy-start.1 = (bf16[64,8,1024]{2,1,0:T(8,128)(2,1)S(1)}, bf16[64,8,1024]{2,1,0:T(8,128)(2,1)}, u32[]{:S(2)}) copy-start(bf16[64,8,1024]{2,1,0:T(8,128)(2,1)} %copy-done) | copy-start | bytes 3145732
  277.0 42.7 %all-to-all-start.5 = ((bf16[8,128,768]{2,1,0:T(8,128)(2,1)}), bf16[8,128,768]{2,1,0:T(8,128)(2,1)}, u32[]{:S(2)}, u32[]{:S(2)}) async-start(bf16[8,128,768]{2,1,0:T(8,128)(2,1)} %bitcast.88), calls=%async_computation.5 | async-start | bytes 3145728 | tf_op jit(solution)/shard_map/all_to_all | solution.py:87
  319.7 42.7 %all-to-all-start.6 = ((bf16[8,128,768]{2,1,0:T(8,128)(2,1)}), bf16[8,128,768]{2,1,0:T(8,128)(2,1)}, u32[]{:S(2)}, u32[]{:S(2)}) async-start(bf16[8,128,768]{2,1,0:T(8,128)(2,1)} %bitcast.87), calls=%async_computation.6 | async-start | bytes 3145728 | tf_op jit(solution)/shard_map/all_to_all | solution.py:88
Sparse Core Ops, SparseCore 0:
  10.1 43.9 all-gather.8
  56.1 41.3 all-gather.6
  99.5 45.4 all-gather.10
where the time goes:
time: 372 us; the launch traced here: 371 us
  waiting for transfers between devices  247 us (66%)
  starting transfers between devices  55.5 us (15%)
  matrix products  28.3 us (8%)
  other arithmetic  14.8 us (4%)
  between operations  14 us (4%)
  local copies, waits for them, and re-layouts  11.9 us (3%)
    all_gather x1, waiting for transfers between devices, per_device(): lax.all_gather(down_weight[0], 'rep', axis=1, tiled=True)  43.9 us
    all_to_all x1, waiting for transfers between devices, per_device(): lax.all_to_all(part_gate, 'rep', split_axis=0, concat_axis=0, tiled=True)  37.2 us
    all_to_all x1, waiting for transfers between devices, per_device(): lax.all_to_all(part_up, 'rep', split_axis=0, concat_axis=0, tiled=True)  34.9 us
    all_gather x1, waiting for transfers between devices, per_device(): lax.all_gather(gate_weight[0], 'rep', axis=0, tiled=True)  28.5 us
    all_to_all x1, waiting for transfers between devices, per_device(): lax.all_to_all(part_down, 'rep', split_axis=0, concat_axis=0, tiled=True)  26.1 us
    all_to_all x1, waiting for transfers between devices, per_device(): lax.all_to_all(output, 'exp', split_axis=0, concat_axis=0, tiled=True)  25.2 us
    all_to_all x1, waiting for transfers between devices, per_device(): lax.all_to_all(grad_rows, 'exp', split_axis=0, concat_axis=0, tiled=True)  25.2 us
    all_to_all x1, waiting for transfers between devices, per_device(): lax.all_to_all(send_rows, 'exp', split_axis=0, concat_axis=0, tiled=True)  23.7 us
  transfers between devices with their start and end apart: 10, of which 8 were waited for; matrix products, arithmetic and copies ran while one was open for 12% of the time, Pallas kernels for 0%

commit v1 on v0

--- a/solution.py
+++ b/solution.py
@@ -2,6 +2,28 @@
 import jax.numpy as jnp
 from jax import lax
 from jax.sharding import PartitionSpec as P
+
+
+def laid_out(blocks, dim):
+    shape = list(blocks.shape[1:])
+    shape[dim] *= blocks.shape[0]
+    return jnp.moveaxis(blocks, 0, dim).reshape(shape)
+
+
+def collect(x, axis, dim):
+    size = lax.axis_size(axis)
+    pairs = [(i, (i + 1) % size) for i in range(size)]
+    back = [(b, a) for a, b in pairs]
+    lower, upper = ([], [])
+    for step in range(size - 1):
+        if step % 2 == 0:
+            lower.append(lax.ppermute(lower[-1] if lower else x, axis, pairs))
+        else:
+            upper.append(lax.ppermute(upper[-1] if upper else x, axis, back))
+    blocks = jnp.stack([*lower[::-1], x, *upper])
+    shift = lax.axis_index(axis) - len(lower)
+    blocks = blocks[(jnp.arange(size) - shift) % size]
+    return laid_out(blocks, dim)
 
 
 def slot_rows(block_ids, expert_count, capacity):
@@ -44,7 +66,7 @@
     w_gate, w_up, w_down = (
         lax.all_gather(gate_weight[0], "rep", axis=0, tiled=True),
         lax.all_gather(up_weight[0], "rep", axis=0, tiled=True),
-        lax.all_gather(down_weight[0], "rep", axis=1, tiled=True),
+        collect(down_weight[0], "rep", 1),
     )
     recv_rows, recv_cot = (
         lax.all_to_all(send_rows, "exp", split_axis=0, concat_axis=0, tiled=True),

time: 372 us -> 341 us (0.917)
  waiting for transfers between devices: 247 us -> 182 us
  starting transfers between devices: 55.5 us -> 81.7 us
  local copies, waits for them, and re-layouts: 11.9 us -> 17.3 us
    all_gather x1 -> x0, waiting for transfers between devices: 43.9 us -> none  [per_device(): lax.all_gather(down_weight[0], 'rep', axis=1, tiled=True)]
    all_gather x1, waiting for transfers between devices: 28.5 us -> 2.34 us  [per_device(): lax.all_gather(gate_weight[0], 'rep', axis=0, tiled=True)]
    all_to_all x1, waiting for transfers between devices: 23.7 us -> 0.01 us  [per_device(): lax.all_to_all(send_rows, 'exp', split_axis=0, concat_axis=0, tiled=True)]
    ppermute x0 -> x7, starting transfers between devices: none -> 23 us  [the longest x3 14 us: collect(): upper.append(lax.ppermute(upper[-1] if upper else x, axis, back))]
    ppermute x0 -> x7, waiting for transfers between devices: none -> 18 us  [the longest x4 17 us: collect(): lower.append(lax.ppermute(lower[-1] if lower else x, axis, pairs))]
    all_to_all x1, waiting for transfers between devices: 0.01 us -> 12.5 us  [per_device(): lax.all_to_all(send_cot, 'exp', split_axis=0, concat_axis=0, tiled=True)]
    all_to_all x1, starting transfers between devices: 15 us -> 6.32 us  [per_device(): lax.all_to_all(grad_rows, 'exp', split_axis=0, concat_axis=0, tiled=True)]
    all_to_all x1, starting transfers between devices: 6.2 us -> 14.3 us  [per_device(): lax.all_to_all(send_cot, 'exp', split_axis=0, concat_axis=0, tiled=True)]
  transfers between devices with their start and end apart: 10 -> 16, of which waited for: 8 -> 10; matrix products, arithmetic and copies ran while one was open for 12% -> 15% of each run, Pallas kernels for 0% -> 0%
where the time goes in v1:
time: 341 us; the launch traced here: 339 us
  waiting for transfers between devices  182 us (53%)
  starting transfers between devices  81.7 us (24%)
  matrix products  28.8 us (8%)
  local copies, waits for them, and re-layouts  17.3 us (5%)
  other arithmetic  14.8 us (4%)
  between operations  14.5 us (4%)
    all_to_all x1, waiting for transfers between devices, per_device(): lax.all_to_all(part_gate, 'rep', split_axis=0, concat_axis=0, tiled=True)  37.3 us
    all_to_all x1, waiting for transfers between devices, per_device(): lax.all_to_all(part_up, 'rep', split_axis=0, concat_axis=0, tiled=True)  34.8 us
    all_to_all x1, waiting for transfers between devices, per_device(): lax.all_to_all(part_down, 'rep', split_axis=0, concat_axis=0, tiled=True)  26.1 us
    all_to_all x1, waiting for transfers between devices, per_device(): lax.all_to_all(grad_rows, 'exp', split_axis=0, concat_axis=0, tiled=True)  25.4 us
    all_to_all x1, waiting for transfers between devices, per_device(): lax.all_to_all(output, 'exp', split_axis=0, concat_axis=0, tiled=True)  25.2 us
    ppermute x4, waiting for transfers between devices, collect(): lower.append(lax.ppermute(lower[-1] if lower else x, axis, pairs))  17 us
    all_to_all x1, starting transfers between devices, per_device(): lax.all_to_all(send_rows, 'exp', split_axis=0, concat_axis=0, tiled=True)  14.8 us
    all_to_all x1, starting transfers between devices, per_device(): lax.all_to_all(send_cot, 'exp', split_axis=0, concat_axis=0, tiled=True)  14.3 us
  transfers between devices with their start and end apart: 16, of which 10 were waited for; matrix products, arithmetic and copies ran while one was open for 15% of the time, Pallas kernels for 0%

profile of v1, /device:TPU:1, one launch (start us, length us, event | category | flops | bytes accessed | tf_op | source)
XLA Modules:
  0.0 339.4 jit_solution(1662494196450764715)
XLA Ops:
  10.8 1.2 broadcast_in_dim.4
  12.4 2.7 scatter_custom_fusion
  15.0 14.8 %all-to-all-start = ((bf16[64,8,1024]{2,1,0:T(8,128)(2,1)}), bf16[64,8,1024]{2,1,0:T(8,128)(2,1)S(1)}, u32[]{:S(2)}, u32[]{:S(2)}) async-start(bf16[64,8,1024]{2,1,0:T(8,128)(2,1)} %bitcast.3), calls=%async_computation | async-start | bytes 2097152 | tf_op jit(solution)/shard_map/all_to_all | solution.py:72
  29.9 3.2 collective-permute-start
  33.2 10.6 %collective-permute-done = bf16[768,128]{1,0:T(8,128)(2,1)S(1)} collective-permute-done((bf16[768,128]{1,0:T(8,128)(2,1)S(1)}, bf16[768,128]{1,0:T(8,128)(2,1)S(1)}, u32[]{:S(2)}, u32[]{:S(2)}) %collective-permute-start) | collective-permute-done | bytes 196640 | tf_op jit(solution)/shard_map/ppermute | solution.py:20
  43.8 1.9 collective-permute-start.1
  45.7 4.6 %collective-permute-start.4 = (bf16[768,128]{1,0:T(8,128)(2,1)S(1)}, bf16[768,128]{1,0:T(8,128)(2,1)}, u32[]{:S(2)}, u32[]{:S(2)}) collective-permute-start(bf16[768,128]{1,0:T(8,128)(2,1)S(1)} %bitcast.104), channel_id=1, source_target_pairs={{64,0},{128,64},{192,128},{256,192},{320,256},{384,320},{448,384},... | collective-permute-start | bytes 589832 | tf_op jit(solution)/shard_map/ppermute | solution.py:22
  50.3 6.4 %collective-permute-done.1 = bf16[768,128]{1,0:T(8,128)(2,1)} collective-permute-done((bf16[768,128]{1,0:T(8,128)(2,1)S(1)}, bf16[768,128]{1,0:T(8,128)(2,1)}, u32[]{:S(2)}, u32[]{:S(2)}) %collective-permute-start.1) | collective-permute-done | bytes 196640 | tf_op jit(solution)/shard_map/ppermute | solution.py:20
  56.7 1.9 collective-permute-start.2
  59.9 2.7 scatter_custom_fusion.1
  62.6 4.6 %collective-permute-start.5 = (bf16[768,128]{1,0:T(8,128)(2,1)}, bf16[768,128]{1,0:T(8,128)(2,1)S(1)}, u32[]{:S(2)}, u32[]{:S(2)}) collective-permute-start(bf16[768,128]{1,0:T(8,128)(2,1)} %collective-permute-done.4), channel_id=1, source_target_pairs={{64,0},{128,64},{192,128},{256,192},{320,256},{384,320},{448,384},... | collective-permute-start | bytes 589832 | tf_op jit(solution)/shard_map/ppermute | solution.py:22
  67.2 1.9 collective-permute-start.3
  69.2 0.9 collective-permute-done.5
  70.1 4.9 %collective-permute-start.6 = (bf16[768,128]{1,0:T(8,128)(2,1)S(1)}, bf16[768,128]{1,0:T(8,128)(2,1)}, u32[]{:S(2)}, u32[]{:S(2)}) collective-permute-start(bf16[768,128]{1,0:T(8,128)(2,1)S(1)} %collective-permute-done.5), channel_id=1, source_target_pairs={{64,0},{128,64},{192,128},{256,192},{320,256},{384,320},{448,384},... | collective-permute-start | bytes 589832 | tf_op jit(solution)/shard_map/ppermute | solution.py:22
  75.1 14.3 %all-to-all-start.2 = ((bf16[64,8,1024]{2,1,0:T(8,128)(2,1)}), bf16[64,8,1024]{2,1,0:T(8,128)(2,1)}, u32[]{:S(2)}, u32[]{:S(2)}) async-start(bf16[64,8,1024]{2,1,0:T(8,128)(2,1)} %bitcast.20), calls=%async_computation.2 | async-start | bytes 2097152 | tf_op jit(solution)/shard_map/all_to_all | solution.py:73
  89.4 1.0 bitcast_dynamic-update-slice_fusion.5
  90.4 1.0 bitcast_dynamic-update-slice_fusion.4
  91.4 1.0 bitcast_dynamic-update-slice_fusion.2
  92.4 1.0 bitcast_dynamic-update-slice_fusion
  93.4 0.9 gather_fusion
  95.0 4.5 %fusion.1 = f32[512,768]{1,0:T(8,128)} fusion(bf16[1,1024,768]{2,1,0:T(8,128)(2,1)} %all-gather.7.cloned.1.call-done, bf16[64,8,1024]{2,1,0:T(8,128)(2,1)} %copy-done.2), kind=kOutput, calls=%fused_computation.13 | convolution fusion | flops 805306368 | bytes 4194304 | tf_op jit(solution)/shard_map/dot_general | solution.py:38
  99.5 2.3 all-gather.5.cloned.1.call-done
  101.8 3.5 %fusion.5 = f32[512,768]{1,0:T(8,128)} fusion(bf16[1,1024,768]{2,1,0:T(8,128)(2,1)} %all-gather.5.cloned.1.call-done, bf16[64,8,1024]{2,1,0:T(8,128)(2,1)S(1)} %copy-done.3), kind=kOutput, calls=%fused_computation.17 | convolution fusion | flops 805306368 | bytes 4194304 | tf_op jit(solution)/shard_map/dot_general | solution.py:37
  105.4 12.5 %all-to-all-done.2 = bf16[64,8,1024]{2,1,0:T(8,128)(2,1)} async-done(((bf16[64,8,1024]{2,1,0:T(8,128)(2,1)}), bf16[64,8,1024]{2,1,0:T(8,128)(2,1)}, u32[]{:S(2)}, u32[]{:S(2)}) %all-to-all-start.2) | async-done | bytes 1048608 | tf_op jit(solution)/shard_map/all_to_all | solution.py:73
  117.9 4.6 %multiply_convert_fusion = (bf16[512,768]{1,0:T(8,128)(2,1)S(1)}, bf16[512,768]{1,0:T(8,128)(2,1)S(1)}, bf16[512,768]{1,0:T(8,128)(2,1)}) fusion(f32[512,768]{1,0:T(8,128)} %fusion.5, f32[512,768]{1,0:T(8,128)} %fusion.1, bf16[768,1024]{0,1:T(8,128)(2,1)S(1)} %bitcast.99, bf16[64,8,1024]{2,1,0:T(8,128)(2,1)} %all-to-all-done.2), kind=kOutput, calls=%fused_computation.19 | convolution fusion | flops 811204608 | bytes 8126464 | tf_op jit(solution)/shard_map/dot_general | solution.py:78
  122.5 1.0 fusion.3
  124.5 2.0 fusion.9
  126.5 6.3 %all-to-all-start.3 = ((bf16[64,8,1024]{2,1,0:T(8,128)(2,1)}), bf16[64,8,1024]{2,1,0:T(8,128)(2,1)S(1)}, u32[]{:S(2)}, u32[]{:S(2)}) async-start(bf16[64,8,1024]{2,1,0:T(8,128)(2,1)} %fusion.9), calls=%async_computation.3 | async-start | bytes 2097152 | tf_op jit(solution)/shard_map/all_to_all | solution.py:96
  132.8 3.1 fusion.8
  135.9 25.4 %all-to-all-done.3 = bf16[64,8,1024]{2,1,0:T(8,128)(2,1)S(1)} async-done(((bf16[64,8,1024]{2,1,0:T(8,128)(2,1)}), bf16[64,8,1024]{2,1,0:T(8,128)(2,1)S(1)}, u32[]{:S(2)}, u32[]{:S(2)}) %all-to-all-start.3) | async-done | bytes 1048608 | tf_op jit(solution)/shard_map/all_to_all | solution.py:96
  161.4 6.2 %all-to-all-start.1 = ((bf16[64,8,1024]{2,1,0:T(8,128)(2,1)}), bf16[64,8,1024]{2,1,0:T(8,128)(2,1)S(1)}, u32[]{:S(2)}, u32[]{:S(2)}) async-start(bf16[64,8,1024]{2,1,0:T(8,128)(2,1)} %fusion.8), calls=%async_computation.1 | async-start | bytes 2097152 | tf_op jit(solution)/shard_map/all_to_all | solution.py:95
  167.6 3.3 convolution_convert_fusion.2
  170.9 25.2 %all-to-all-done.1 = bf16[64,8,1024]{2,1,0:T(8,128)(2,1)S(1)} async-done(((bf16[64,8,1024]{2,1,0:T(8,128)(2,1)}), bf16[64,8,1024]{2,1,0:T(8,128)(2,1)S(1)}, u32[]{:S(2)}, u32[]{:S(2)}) %all-to-all-start.1) | async-done | bytes 1048608 | tf_op jit(solution)/shard_map/all_to_all | solution.py:95
  196.1 8.0 %all-to-all-start.4 = ((bf16[8,128,768]{2,1,0:T(8,128)(2,1)}), bf16[8,128,768]{2,1,0:T(8,128)(2,1)}, u32[]{:S(2)}, u32[]{:S(2)}) async-start(bf16[8,128,768]{2,1,0:T(8,128)(2,1)} %bitcast.102), calls=%async_computation.4 | async-start | bytes 3145728 | tf_op jit(solution)/shard_map/all_to_all | solution.py:108
  204.1 3.3 convolution_convert_fusion.1
  207.4 37.3 %all-to-all-done.4 = bf16[8,128,768]{2,1,0:T(8,128)(2,1)} async-done(((bf16[8,128,768]{2,1,0:T(8,128)(2,1)}), bf16[8,128,768]{2,1,0:T(8,128)(2,1)}, u32[]{:S(2)}, u32[]{:S(2)}) %all-to-all-start.4) | async-done | bytes 1572896 | tf_op jit(solution)/shard_map/all_to_all | solution.py:108
  244.7 4.4 %all-to-all-start.5 = ((bf16[8,128,768]{2,1,0:T(8,128)(2,1)}), bf16[8,128,768]{2,1,0:T(8,128)(2,1)}, u32[]{:S(2)}, u32[]{:S(2)}) async-start(bf16[8,128,768]{2,1,0:T(8,128)(2,1)} %bitcast.101), calls=%async_computation.5 | async-start | bytes 3145728 | tf_op jit(solution)/shard_map/all_to_all | solution.py:109
  249.1 3.4 %convolution_convert_fusion = bf16[1024,768]{1,0:T(8,128)(2,1)} fusion(bf16[512,768]{1,0:T(8,128)(2,1)S(1)} %copy-done.14, bf16[64,8,1024]{2,1,0:T(8,128)(2,1)} %all-to-all-done.2), kind=kOutput, calls=%fused_computation.9 | convolution fusion | flops 806092800 | bytes 3407872 | tf_op jit(solution)/shard_map/dot_general | solution.py:104
  252.5 34.8 %all-to-all-done.5 = bf16[8,128,768]{2,1,0:T(8,128)(2,1)} async-done(((bf16[8,128,768]{2,1,0:T(8,128)(2,1)}), bf16[8,128,768]{2,1,0:T(8,128)(2,1)}, u32[]{:S(2)}, u32[]{:S(2)}) %all-to-all-start.5) | async-done | bytes 1572896 | tf_op jit(solution)/shard_map/all_to_all | solution.py:109
  287.4 4.5 %all-to-all-start.6 = ((bf16[8,128,768]{2,1,0:T(8,128)(2,1)}), bf16[8,128,768]{2,1,0:T(8,128)(2,1)}, u32[]{:S(2)}, u32[]{:S(2)}) async-start(bf16[8,128,768]{2,1,0:T(8,128)(2,1)} %bitcast.98), calls=%async_computation.6 | async-start | bytes 3145728 | tf_op jit(solution)/shard_map/all_to_all | solution.py:110
  291.9 1.2 gather_fusion.2
  293.3 2.1 reduce_sum.62
  295.4 1.2 gather_fusion.1
  297.2 2.1 multiply_reduce_fusion
  299.3 1.7 convert_reduce_fusion.2
  300.9 1.7 convert_reduce_fusion.1
  304.0 26.1 %all-to-all-done.6 = bf16[8,128,768]{2,1,0:T(8,128)(2,1)} async-done(((bf16[8,128,768]{2,1,0:T(8,128)(2,1)}), bf16[8,128,768]{2,1,0:T(8,128)(2,1)}, u32[]{:S(2)}, u32[]{:S(2)}) %all-to-all-start.6) | async-done | bytes 1572896 | tf_op jit(solution)/shard_map/all_to_all | solution.py:110
  330.1 1.7 convert_reduce_fusion
  (72 shorter events, 10.2 us)
Async XLA Ops:
  7.2 87.8 %all-gather.7.cloned.1.call-start = ((), (), s32[]{:S(2)}) async-start(), calls=%async_computation.8 | async-start | bytes 1769472 | tf_op jit(solution)/shard_map/all_gather | solution.py:68
  12.3 17.6 %copy-start.6 = (bf16[1,768,128]{2,1,0:T(8,128)(2,1)S(1)}, bf16[1,768,128]{2,1,0:T(8,128)(2,1)}, u32[]{:S(2)}) copy-start(bf16[1,768,128]{2,1,0:T(8,128)(2,1)} %param.13) | copy-start | bytes 589828
  12.3 46.3 %copy-start.9 = (f32[128,2]{0,1:T(2,128)S(1)}, f32[128,2]{0,1:T(2,128)}, u32[]{:S(2)}) copy-start(f32[128,2]{0,1:T(2,128)} %param.10) | copy-start | bytes 3076
  12.3 46.5 %copy-start.5 = (bf16[128,1024]{1,0:T(8,128)(2,1)S(1)}, bf16[128,1024]{1,0:T(8,128)(2,1)}, u32[]{:S(2)}) copy-start(bf16[128,1024]{1,0:T(8,128)(2,1)} %param.8) | copy-start | bytes 786436
  15.0 60.0 %all-to-all-start = ((bf16[64,8,1024]{2,1,0:T(8,128)(2,1)}), bf16[64,8,1024]{2,1,0:T(8,128)(2,1)S(1)}, u32[]{:S(2)}, u32[]{:S(2)}) async-start(bf16[64,8,1024]{2,1,0:T(8,128)(2,1)} %bitcast.3), calls=%async_computation | async-start | bytes 2097152 | tf_op jit(solution)/shard_map/all_to_all | solution.py:72
  29.9 71.9 %all-gather.5.cloned.1.call-start = ((), (), s32[]{:S(2)}) async-start(), calls=%async_computation.7 | async-start | bytes 1769472 | tf_op jit(solution)/shard_map/all_gather | solution.py:67
  29.9 13.9 %collective-permute-start = (bf16[768,128]{1,0:T(8,128)(2,1)S(1)}, bf16[768,128]{1,0:T(8,128)(2,1)S(1)}, u32[]{:S(2)}, u32[]{:S(2)}) collective-permute-start(bf16[768,128]{1,0:T(8,128)(2,1)S(1)} %bitcast.103), channel_id=1, source_target_pairs={{0,64},{64,128},{128,192},{192,256},{256,320},{320,384},{384,448},... | collective-permute-start | bytes 589832 | tf_op jit(solution)/shard_map/ppermute | solution.py:20
  43.8 15.1 %copy-start.7 = (bf16[768,128]{1,0:T(8,128)(2,1)}, bf16[768,128]{1,0:T(8,128)(2,1)S(1)}, u32[]{:S(2)}) copy-start(bf16[768,128]{1,0:T(8,128)(2,1)S(1)} %collective-permute-done) | copy-start | bytes 589828
  43.8 12.9 %collective-permute-start.1 = (bf16[768,128]{1,0:T(8,128)(2,1)S(1)}, bf16[768,128]{1,0:T(8,128)(2,1)}, u32[]{:S(2)}, u32[]{:S(2)}) collective-permute-start(bf16[768,128]{1,0:T(8,128)(2,1)S(1)} %collective-permute-done), channel_id=1, source_target_pairs={{0,64},{64,128},{128,192},{192,256},{256,320},{320,384},{384,448},... | collective-permute-start | bytes 589832 | tf_op jit(solution)/shard_map/ppermute | solution.py:20
  45.7 16.9 %collective-permute-start.4 = (bf16[768,128]{1,0:T(8,128)(2,1)S(1)}, bf16[768,128]{1,0:T(8,128)(2,1)}, u32[]{:S(2)}, u32[]{:S(2)}) collective-permute-start(bf16[768,128]{1,0:T(8,128)(2,1)S(1)} %bitcast.104), channel_id=1, source_target_pairs={{64,0},{128,64},{192,128},{256,192},{320,256},{384,320},{448,384},... | collective-permute-start | bytes 589832 | tf_op jit(solution)/shard_map/ppermute | solution.py:22
  56.7 10.5 %collective-permute-start.2 = (bf16[768,128]{1,0:T(8,128)(2,1)}, bf16[768,128]{1,0:T(8,128)(2,1)}, u32[]{:S(2)}, u32[]{:S(2)}) collective-permute-start(bf16[768,128]{1,0:T(8,128)(2,1)} %collective-permute-done.1), channel_id=1, source_target_pairs={{0,64},{64,128},{128,192},{192,256},{256,320},{320,384},{384,448},... | collective-permute-start | bytes 589832 | tf_op jit(solution)/shard_map/ppermute | solution.py:20
  62.6 7.5 %collective-permute-start.5 = (bf16[768,128]{1,0:T(8,128)(2,1)}, bf16[768,128]{1,0:T(8,128)(2,1)S(1)}, u32[]{:S(2)}, u32[]{:S(2)}) collective-permute-start(bf16[768,128]{1,0:T(8,128)(2,1)} %collective-permute-done.4), channel_id=1, source_target_pairs={{64,0},{128,64},{192,128},{256,192},{320,256},{384,320},{448,384},... | collective-permute-start | bytes 589832 | tf_op jit(solution)/shard_map/ppermute | solution.py:22
  67.2 7.8 %collective-permute-start.3 = (bf16[768,128]{1,0:T(8,128)(2,1)}, bf16[768,128]{1,0:T(8,128)(2,1)S(1)}, u32[]{:S(2)}, u32[]{:S(2)}) collective-permute-start(bf16[768,128]{1,0:T(8,128)(2,1)} %collective-permute-done.2), channel_id=1, source_target_pairs={{0,64},{64,128},{128,192},{192,256},{256,320},{320,384},{384,448},... | collective-permute-start | bytes 589832 | tf_op jit(solution)/shard_map/ppermute | solution.py:20
  69.2 22.2 %copy-start.8 = (bf16[768,128]{1,0:T(8,128)(2,1)S(1)}, bf16[768,128]{1,0:T(8,128)(2,1)}, u32[]{:S(2)}) copy-start(bf16[768,128]{1,0:T(8,128)(2,1)} %copy-done.7) | copy-start | bytes 589828
  70.1 22.3 %collective-permute-start.6 = (bf16[768,128]{1,0:T(8,128)(2,1)S(1)}, bf16[768,128]{1,0:T(8,128)(2,1)}, u32[]{:S(2)}, u32[]{:S(2)}) collective-permute-start(bf16[768,128]{1,0:T(8,128)(2,1)S(1)} %collective-permute-done.5), channel_id=1, source_target_pairs={{64,0},{128,64},{192,128},{256,192},{320,256},{384,320},{448,384},... | collective-permute-start | bytes 589832 | tf_op jit(solution)/shard_map/ppermute | solution.py:22
  75.1 16.3 %copy-start.2 = (bf16[64,8,1024]{2,1,0:T(8,128)(2,1)}, bf16[64,8,1024]{2,1,0:T(8,128)(2,1)S(1)}, u32[]{:S(2)}) copy-start(bf16[64,8,1024]{2,1,0:T(8,128)(2,1)S(1)} %all-to-all-done) | copy-start | bytes 3145732
  75.1 42.8 %all-to-all-start.2 = ((bf16[64,8,1024]{2,1,0:T(8,128)(2,1)}), bf16[64,8,1024]{2,1,0:T(8,128)(2,1)}, u32[]{:S(2)}, u32[]{:S(2)}) async-start(bf16[64,8,1024]{2,1,0:T(8,128)(2,1)} %bitcast.20), calls=%async_computation.2 | async-start | bytes 2097152 | tf_op jit(solution)/shard_map/all_to_all | solution.py:73
  95.0 22.9 %copy-start = (bf16[768,8,128]{0,2,1:T(8,128)(2,1)}, bf16[768,8,128]{0,2,1:T(8,128)(2,1)S(1)}, u32[]{:S(2)}) copy-start(bf16[768,8,128]{0,2,1:T(8,128)(2,1)S(1)} %copy.25) | copy-start | bytes 4718596
  95.0 6.8 %copy-start.3 = (bf16[64,8,1024]{2,1,0:T(8,128)(2,1)S(1)}, bf16[64,8,1024]{2,1,0:T(8,128)(2,1)}, u32[]{:S(2)}) copy-start(bf16[64,8,1024]{2,1,0:T(8,128)(2,1)} %copy-done.2) | copy-start | bytes 3145732
  117.9 4.6 %copy-start.11 = (bf16[1,1024,768]{2,1,0:T(8,128)(2,1)S(1)}, bf16[1,1024,768]{2,1,0:T(8,128)(2,1)}, u32[]{:S(2)}) copy-start(bf16[1,1024,768]{2,1,0:T(8,128)(2,1)} %all-gather.5.cloned.1.call-done) | copy-start | bytes 4718596
  122.5 1.0 copy-start.13
  122.5 1.2 copy-start.12
  122.5 2.0 copy-start.10
  126.5 6.3 %copy-start.1 = (bf16[768,8,128]{0,2,1:T(8,128)(2,1)S(1)}, bf16[768,8,128]{0,2,1:T(8,128)(2,1)}, u32[]{:S(2)}) copy-start(bf16[768,8,128]{0,2,1:T(8,128)(2,1)} %copy-done) | copy-start | bytes 4718596
  126.5 34.9 %all-to-all-start.3 = ((bf16[64,8,1024]{2,1,0:T(8,128)(2,1)}), bf16[64,8,1024]{2,1,0:T(8,128)(2,1)S(1)}, u32[]{:S(2)}, u32[]{:S(2)}) async-start(bf16[64,8,1024]{2,1,0:T(8,128)(2,1)} %fusion.9), calls=%async_computation.3 | async-start | bytes 2097152 | tf_op jit(solution)/shard_map/all_to_all | solution.py:96
  135.9 31.6 %copy-start.4 = (bf16[64,8,1024]{2,1,0:T(8,128)(2,1)S(1)}, bf16[64,8,1024]{2,1,0:T(8,128)(2,1)}, u32[]{:S(2)}) copy-start(bf16[64,8,1024]{2,1,0:T(8,128)(2,1)} %copy-done.2) | copy-start | bytes 3145732
  161.4 34.8 %all-to-all-start.1 = ((bf16[64,8,1024]{2,1,0:T(8,128)(2,1)}), bf16[64,8,1024]{2,1,0:T(8,128)(2,1)S(1)}, u32[]{:S(2)}, u32[]{:S(2)}) async-start(bf16[64,8,1024]{2,1,0:T(8,128)(2,1)} %fusion.8), calls=%async_computation.1 | async-start | bytes 2097152 | tf_op jit(solution)/shard_map/all_to_all | solution.py:95
  196.1 48.6 %all-to-all-start.4 = ((bf16[8,128,768]{2,1,0:T(8,128)(2,1)}), bf16[8,128,768]{2,1,0:T(8,128)(2,1)}, u32[]{:S(2)}, u32[]{:S(2)}) async-start(bf16[8,128,768]{2,1,0:T(8,128)(2,1)} %bitcast.102), calls=%async_computation.4 | async-start | bytes 3145728 | tf_op jit(solution)/shard_map/all_to_all | solution.py:108
  244.7 4.4 %copy-start.14 = (bf16[512,768]{1,0:T(8,128)(2,1)S(1)}, bf16[512,768]{1,0:T(8,128)(2,1)}, u32[]{:S(2)}) copy-start(bf16[512,768]{1,0:T(8,128)(2,1)} %get-tuple-element.17) | copy-start | bytes 2359300
  244.7 42.7 %all-to-all-start.5 = ((bf16[8,128,768]{2,1,0:T(8,128)(2,1)}), bf16[8,128,768]{2,1,0:T(8,128)(2,1)}, u32[]{:S(2)}, u32[]{:S(2)}) async-start(bf16[8,128,768]{2,1,0:T(8,128)(2,1)} %bitcast.101), calls=%async_computation.5 | async-start | bytes 3145728 | tf_op jit(solution)/shard_map/all_to_all | solution.py:109
  287.4 42.7 %all-to-all-start.6 = ((bf16[8,128,768]{2,1,0:T(8,128)(2,1)}), bf16[8,128,768]{2,1,0:T(8,128)(2,1)}, u32[]{:S(2)}, u32[]{:S(2)}) async-start(bf16[8,128,768]{2,1,0:T(8,128)(2,1)} %bitcast.98), calls=%async_computation.6 | async-start | bytes 3145728 | tf_op jit(solution)/shard_map/all_to_all | solution.py:110
Sparse Core Ops, SparseCore 0:
  10.1 48.6 all-gather.6
  60.9 40.8 all-gather.4
